TPU v7x, 128 devices: a whole 4x4x4 slice. The times are simulated.
128 devices in a mesh: sec: 2 (over core), dev: 64 (over z, x, y).
Axes of the slice: x: 4, y: 4, z: 4, core: 2. Of those that a mesh axis runs over, the one named last changes fastest.
Arguments:
- queries: bfloat16 [256, 4, 6144], P('dev'), may hold values from -160 to 160
- cache_keys: bfloat16 [256, 128, 1024], P('dev'), may hold values from -8 to 8
- cache_values: bfloat16 [256, 128, 1024], P('dev'), may hold values from -6 to 6
- lengths: int32 [256], P('dev'), may hold values from 1 to 128, 16384 in all
- new_keys: bfloat16 [256, 4, 1024], P('dev'), may hold values from -6 to 6
- new_values: bfloat16 [256, 4, 1024], P('dev'), may hold values from -6 to 6
- residual: bfloat16 [256, 4, 6144], P('dev'), may hold values from -6 to 6
- norm_gain: float32 [6144], replicated, may hold values from 0.25 to 1.75
- expert_ids: int32 [1024, 2], P('dev'), may hold values from 0 to 3, all different within a row; in each aligned block of 16 rows (0 to 15, 16 to 31, ...) at most 9 rows name the same one
- gate_logits: float32 [1024, 2], P('dev'), may hold values from -8 to 8
- w_gate: bfloat16 [6144, 32768], P(None, 'dev'), may hold values from -0.078125 to 0.078125
- w_up: bfloat16 [6144, 32768], P(None, 'dev'), may hold values from -0.078125 to 0.078125
- w_down: bfloat16 [32768, 6144], P('dev'), may hold values from -0.0625 to 0.0625
Outputs:
- layer_out: bfloat16 [256, 4, 6144], P('dev', None, 'sec')
Inputs may be any that keep to these rules, and one draw needn't show every extreme that they name: `expert_ids`: in the 16 tokens of one attention device no expert is named more than 9 times; some expert is named exactly 9 times in some of these blocks.
All inputs are finite; a program needn't handle non-finite values. No bound on the sum of `lengths` on one device may be relied on, other than what follows from the above.
Results may differ from a plain program's by a relative error of at most 0.0065.
Values may be sent and summed in bfloat16 or wider, within the bound.
A program may use at most 192 MiB of HBM per device.

v0:
```python
import jax
import jax.numpy as jnp
from jax import lax
from jax.sharding import PartitionSpec as P

HEADS = 48
KVH = 8
HD = 128
EXP = 4
LMAX = 128
CAP = 9
epsilon = 1e-05


def from_behind(x, axis, by):
    size = lax.axis_size(axis)
    pairs = [(i, i + by) for i in range(size) if 0 <= i + by < size]
    return lax.ppermute(x, axis, pairs)


def attend_local(operands):
    queries, cache_keys, cache_values, lengths, new_keys, new_values, residual, norm_gain = operands
    requests = queries.shape[0]
    steps = queries.shape[1]
    width = residual.shape[2]
    per_group = HEADS // KVH
    key_all = jnp.concatenate([cache_keys, new_keys], axis=1).reshape(
        requests, LMAX + steps, KVH, HD
    )
    value_all = jnp.concatenate([cache_values, new_values], axis=1).reshape(
        requests, LMAX + steps, KVH, HD
    )
    query_heads = queries.reshape(requests, steps, KVH, per_group, HD)
    scores = jnp.einsum(
        "rsgqd,rlgd->rsgql", query_heads, key_all, preferred_element_type=jnp.float32
    ) * HD ** (-0.5)
    position = jnp.arange(LMAX + steps, dtype=jnp.int32)
    stepnum = jnp.arange(steps, dtype=jnp.int32)
    in_cache = position[None, None, :] < lengths[:, None, None]
    in_window = (position[None, :] >= LMAX) & (position[None, :] - LMAX <= stepnum[:, None])
    valid = in_cache | in_window[None, :, :]
    scores = jnp.where(valid[:, :, None, None, :], scores, jnp.float32(-1e30))
    peak = jnp.max(scores, axis=-1, keepdims=True)
    expo = jnp.exp(scores - peak)
    probs = (expo / jnp.sum(expo, axis=-1, keepdims=True)).astype(jnp.bfloat16)
    attended = jnp.einsum("rsgql,rlgd->rsgqd", probs, value_all, preferred_element_type=jnp.float32)
    attended = attended.reshape(requests, steps, width)
    hstate = (residual.astype(jnp.float32) + attended).astype(jnp.bfloat16)
    hfloat = hstate.astype(jnp.float32)
    meansq = jnp.mean(hfloat * hfloat, axis=-1, keepdims=True)
    normed = (hfloat * lax.rsqrt(meansq + epsilon) * norm_gain).astype(jnp.bfloat16)
    return (hstate, normed)


def attend_skip(operands):
    residual = operands[6]
    return (jnp.zeros_like(residual), jnp.zeros_like(residual))


def expert_rows(rows, w_gate, w_up, w_down):
    gate = jnp.dot(rows, w_gate, preferred_element_type=jnp.float32)
    upward = jnp.dot(rows, w_up, preferred_element_type=jnp.float32)
    hidden = (jax.nn.silu(gate) * upward).astype(jnp.bfloat16)
    return jnp.dot(hidden, w_down, preferred_element_type=jnp.float32).astype(jnp.bfloat16)


def shards(
    queries,
    cache_keys,
    cache_values,
    lengths,
    new_keys,
    new_values,
    residual,
    norm_gain,
    expert_ids,
    gate_logits,
    w_gate,
    w_up,
    w_down,
):
    is_attention = lax.axis_index("sec") == 0
    is_expert = jnp.logical_not(is_attention)
    devices = lax.axis_size("dev")
    group = devices // EXP
    my_expert = lax.axis_index("dev") // group
    requests = residual.shape[0]
    steps = residual.shape[1]
    width = residual.shape[2]
    half = width // 2
    tok_rows = requests * steps
    operands = (
        queries,
        cache_keys,
        cache_values,
        lengths,
        new_keys,
        new_values,
        residual,
        norm_gain,
    )
    hstate, normed = lax.cond(is_attention, attend_local, attend_skip, operands)
    flat_h = hstate.reshape(tok_rows, width)
    flat_in = normed.reshape(tok_rows, width)
    flat_ids = expert_ids.reshape(-1)
    onehot = (flat_ids[:, None] == jnp.arange(EXP, dtype=jnp.int32)[None, :]).astype(jnp.int32)
    ranks = jnp.cumsum(onehot, axis=0) - onehot
    slot_of = jnp.sum(ranks * onehot, axis=1)
    target = (flat_ids * CAP + slot_of).reshape(tok_rows, 2)
    slot_rows = jnp.arange(EXP * CAP, dtype=jnp.int32)
    first_hit = target[:, 0:1] == slot_rows[None, :]
    second_hit = target[:, 1:2] == slot_rows[None, :]
    placing = jnp.logical_or(first_hit, second_hit).astype(jnp.bfloat16)
    buffer = lax.dot_general(
        placing, flat_in, (((0,), (0,)), ((), ())), preferred_element_type=jnp.float32
    )
    buffer = buffer.astype(jnp.bfloat16).reshape(EXP, CAP, width)
    weights = jax.nn.softmax(gate_logits, axis=-1)
    mixing = weights[:, 0:1] * first_hit.astype(jnp.float32) + weights[:, 1:2] * second_hit.astype(
        jnp.float32
    )
    moved_rows, moved_high = from_behind((buffer, flat_h[:, half:]), "sec", 1)
    mine = lax.dynamic_index_in_dim(
        lax.all_gather(moved_rows, "dev", axis=1, tiled=True), my_expert, 0, keepdims=False
    )
    partials = lax.cond(
        is_expert,
        lambda block: expert_rows(block, w_gate, w_up, w_down),
        lambda block: jnp.zeros_like(block),
        mine,
    )
    partials = partials.reshape(devices, CAP, width)
    returned = lax.all_to_all(partials, "dev", split_axis=0, concat_axis=0, tiled=True)
    summed = jnp.sum(returned.reshape(EXP, group, CAP, width).astype(jnp.float32), axis=1)
    mixed = jnp.dot(
        mixing,
        summed.reshape(EXP * CAP, width),
        precision=lax.Precision.HIGHEST,
        preferred_element_type=jnp.float32,
    )
    upper_out = (moved_high.astype(jnp.float32) + mixed[:, half:]).astype(jnp.bfloat16)
    lower_mix = from_behind(mixed[:, :half], "sec", -1)
    lower_out = (flat_h[:, :half].astype(jnp.float32) + lower_mix).astype(jnp.bfloat16)
    layer_out = jnp.where(is_attention, lower_out, upper_out)
    return layer_out.reshape(requests, steps, half)


def solution(mesh):
    return jax.shard_map(
        shards,
        mesh=mesh,
        in_specs=(
            P("dev", None, None),
            P("dev", None, None),
            P("dev", None, None),
            P("dev"),
            P("dev", None, None),
            P("dev", None, None),
            P("dev", None, None),
            P(),
            P("dev", None),
            P("dev", None),
            P(None, "dev"),
            P(None, "dev"),
            P("dev", None),
        ),
        out_specs=P("dev", None, "sec"),
        check_vma=False,
    )
```

profile of v0, /device:TPU:25, one launch (start us, length us, event | category | flops | bytes accessed | tf_op | source)
XLA Modules:
  0.0 403.3 jit_solution(4926750830387768052)
XLA Ops:
  6.5 0.8 copy.52
  7.9 0.7 multiply_add_fusion
  8.6 0.8 conditional.2
  8.6 0.7 broadcast.102
  9.3 0.4 convolution_convert_fusion.1
  10.3 1.3 collective-permute-start
  11.6 11.2 %collective-permute-done = bf16[4,9,6144]{2,0,1:T(4,128)(2,1)S(1)} collective-permute-done((bf16[4,9,6144]{2,0,1:T(4,128)(2,1)S(1)}, bf16[4,9,6144]{2,0,1:T(4,128)(2,1)S(1)}, u32[]{:S(2)}, u32[]{:S(2)}) %collective-permute-start) | collective-permute-done | bytes 442400 | tf_op jit(solution)/shard_map/ppermute | solution.py:18
  22.8 0.8 copy-done
  23.6 144.2 %all-gather.2.cloned.1.call-done = bf16[4,576,6144]{2,0,1:T(4,128)(2,1)} async-done(((bf16[4,9,6144]{2,0,1:T(4,128)(2,1)}), bf16[4,576,6144]{2,0,1:T(4,128)(2,1)}) %all-gather.2.cloned.1.call-update) | async-done | bytes 28311568 | tf_op jit(solution)/shard_map/all_gather | solution.py:124
  167.8 41.2 %conditional.3 = (bf16[576,6144]{1,0:T(8,128)(2,1)}) conditional(s32[]{:T(128)} %convert_element_type.63, () %tuple.38, (s32[]{:T(128)}, s32[]{:T(128)}, s32[]{:T(128)}, bf16[4,576,6144]{2,0,1:T(4,128)(2,1)}, bf16[6144,512]{1,0:T(8,128)(2,1)}, /*index=5*/bf16[6144,512]{1,0:T(8,128)(2,1)}, bf16[512,6144]{1,0:T(8,128)(2,1)}, s32[]{:T(128)}) %tuple.40), branch_computations={%region_9.10_spmd, %region_10.11_spmd.clone} | conditional | flops 10876944384 | bytes 144310560 | solution.py:126
  167.8 20.3 %copy.55 = bf16[4,576,6144]{2,1,0:T(8,128)(2,1)} copy(bf16[4,576,6144]{2,0,1:T(4,128)(2,1)} %get-tuple-element.212) | data formatting | bytes 56623104 | tf_op jit(solution)/shard_map
  188.1 8.0 %fusion.15 = f32[576,512]{1,0:T(8,128)S(1)} fusion(bf16[6144,512]{1,0:T(8,128)(2,1)} %get-tuple-element.190, bf16[4,576,6144]{2,1,0:T(8,128)(2,1)} %copy.55, s32[]{:T(128)S(6)} %select_n.31), kind=kOutput, calls=%fused_computation.30 | convolution fusion | flops 3623878656 | bytes 14548996 | tf_op jit(solution)/shard_map/cond/branch_1_fun/dot_general | solution.py:61
  196.1 6.9 %fusion.22 = bf16[576,512]{1,0:T(8,128)(2,1)S(1)} fusion(bf16[6144,512]{1,0:T(8,128)(2,1)S(1)} %copy-done.5, bf16[4,576,6144]{2,1,0:T(8,128)(2,1)} %copy.55, s32[]{:T(128)S(6)} %select_n.31, f32[576,512]{1,0:T(8,128)S(1)} %fusion.15), kind=kOutput, calls=%fused_computation.35 | convolution fusion | flops 3625648128 | bytes 15138820 | tf_op jit(solution)/shard_map/cond/branch_1_fun/dot_general | solution.py:62
  203.1 6.0 %convolution_convert_fusion = bf16[576,6144]{1,0:T(8,128)(2,1)} fusion(bf16[576,512]{1,0:T(8,128)(2,1)S(1)} %fusion.22, bf16[512,6144]{1,0:T(8,128)(2,1)S(1)} %bitcast.39), kind=kOutput, calls=%fused_computation.27 | convolution fusion | flops 3627417600 | bytes 13959168 | tf_op jit(solution)/shard_map/cond/branch_1_fun/dot_general | solution.py:64
  209.0 10.2 %reshape.123 = bf16[64,9,6144]{2,1,0:T(8,128)(2,1)} reshape(bf16[576,6144]{1,0:T(8,128)(2,1)} %get-tuple-element.235) | data formatting | bytes 14155776 | tf_op jit(solution)/shard_map/reshape | solution.py:132
  219.3 8.4 %all-to-all-start = ((bf16[64,9,6144]{2,1,0:T(8,128)(2,1)}), bf16[64,9,6144]{2,1,0:T(8,128)(2,1)}, u32[]{:S(2)}, u32[]{:S(2)}) async-start(bf16[64,9,6144]{2,1,0:T(8,128)(2,1)} %reshape.123), calls=%async_computation | async-start | bytes 25165824 | tf_op jit(solution)/shard_map/all_to_all | solution.py:133
  227.8 154.7 %all-to-all-done = bf16[64,9,6144]{2,1,0:T(8,128)(2,1)} async-done(((bf16[64,9,6144]{2,1,0:T(8,128)(2,1)}), bf16[64,9,6144]{2,1,0:T(8,128)(2,1)}, u32[]{:S(2)}, u32[]{:S(2)}) %all-to-all-start) | async-done | bytes 7077920 | tf_op jit(solution)/shard_map/all_to_all | solution.py:133
  382.5 6.8 %convert_reduce_fusion = f32[4,9,6144]{2,1,0:T(8,128)S(1)} fusion(bf16[64,9,6144]{2,1,0:T(8,128)(2,1)} %all-to-all-done), kind=kLoop, calls=%fused_computation.38 | loop fusion | flops 6856704 | bytes 7962624 | tf_op jit(solution)/shard_map/reduce_sum | solution.py:134
  389.5 0.7 fusion.30
  390.2 1.3 collective-permute-start.1
  391.5 1.0 reshape.121
  392.5 1.3 collective-permute-start.2
  393.8 1.9 collective-permute-done.2
  395.7 0.7 reshape.125
  (31 shorter events, 1.4 us)
Async XLA Ops:
  6.5 161.3 %all-gather.2.cloned.1.call-start = ((), (), s32[]{:S(2)}) async-start(), calls=%async_computation.1 | async-start | bytes 28753920 | tf_op jit(solution)/shard_map/all_gather | solution.py:124
  10.3 12.5 %collective-permute-start = (bf16[4,9,6144]{2,0,1:T(4,128)(2,1)S(1)}, bf16[4,9,6144]{2,0,1:T(4,128)(2,1)S(1)}, u32[]{:S(2)}, u32[]{:S(2)}) collective-permute-start(bf16[4,9,6144]{2,0,1:T(4,128)(2,1)S(1)} %copy.54), channel_id=1, source_target_pairs={{0,64},{1,65},{2,66},{3,67},{4,68},{5,69},{6,70},{7,71},{8,72},{9,... | collective-permute-start | bytes 1327112 | tf_op jit(solution)/shard_map/ppermute | solution.py:18
  22.8 0.8 copy-start
  167.8 35.2 %slice-start = ((s8[6291456]{0:T(1024)(128)(4,1)}), s8[2097152]{0:T(1024)(128)(4,1)S(1)}, s32[]{:S(2)}) async-start(s8[6291456]{0:T(1024)(128)(4,1)} %bitcast.38), calls=%async_computation.2 | async-start | bytes 4194304 | tf_op jit(solution)/shard_map/cond
  188.1 8.0 %copy-start.5 = (bf16[6144,512]{1,0:T(8,128)(2,1)S(1)}, bf16[6144,512]{1,0:T(8,128)(2,1)}, u32[]{:S(2)}) copy-start(bf16[6144,512]{1,0:T(8,128)(2,1)} %get-tuple-element.191) | copy-start | bytes 18874372 | tf_op jit(solution)/shard_map/cond
  188.1 15.0 %slice-start.1 = ((s8[6291456]{0:T(1024)(128)(4,1)}), s8[4194304]{0:T(1024)(128)(4,1)S(1)}, s32[]{:S(2)}) async-start(s8[6291456]{0:T(1024)(128)(4,1)} %bitcast.38), calls=%async_computation.3 | async-start | bytes 8388608 | tf_op jit(solution)/shard_map/cond
  219.3 8.4 %copy-start.4 = (f32[16,2]{0,1:T(2,128)S(1)}, f32[16,2]{0,1:T(2,128)}, u32[]{:S(2)}) copy-start(f32[16,2]{0,1:T(2,128)} %param.26) | copy-start | bytes 388
  219.3 163.2 %all-to-all-start = ((bf16[64,9,6144]{2,1,0:T(8,128)(2,1)}), bf16[64,9,6144]{2,1,0:T(8,128)(2,1)}, u32[]{:S(2)}, u32[]{:S(2)}) async-start(bf16[64,9,6144]{2,1,0:T(8,128)(2,1)} %reshape.123), calls=%async_computation | async-start | bytes 25165824 | tf_op jit(solution)/shard_map/all_to_all | solution.py:133
  390.2 5.5 %collective-permute-start.1 = (f32[16,3072]{1,0:T(8,128)S(1)}, f32[16,3072]{1,0:T(8,128)S(1)}, u32[]{:S(2)}, u32[]{:S(2)}) collective-permute-start(f32[16,3072]{1,0:T(8,128)S(1)} %slice.33), channel_id=1, source_target_pairs={{64,0},{65,1},{66,2},{67,3},{68,4},{69,5},{70,6},{71,7},{72,8},{73... | collective-permute-start | bytes 589832 | tf_op jit(solution)/shard_map/ppermute | solution.py:18
  392.5 3.2 collective-permute-start.2
Sparse Core Ops, SparseCore 0:
  23.7 144.0 all-gather.1
where the time goes:
time: 404 us; the launch traced here: 403 us
  waiting for transfers between devices  312 us (77%)
  local copies, waits for them, and re-layouts  35.4 us (9%)
  matrix products  22 us (5%)
  between operations  13.5 us (3%)
  starting transfers between devices  12.3 us (3%)
  other arithmetic  7.96 us (2%)
    all_to_all x1, waiting for transfers between devices, shards(): lax.all_to_all(partials, 'dev', split_axis=0, concat_axis=0, tiled=True)  155 us
    all_gather x1, waiting for transfers between devices, shards(): lax.all_gather(moved_rows, 'dev', axis=1, tiled=True)  144 us
    another operation x2, local copies, waits for them, and re-layouts  21 us
    ppermute x3, waiting for transfers between devices, from_behind(): return lax.ppermute(x, axis, pairs)  13.1 us
    reshape x1, local copies, waits for them, and re-layouts, shards(): partials = partials.reshape(devices, CAP, width)  10.2 us
    all_to_all x1, starting transfers between devices, shards(): lax.all_to_all(partials, 'dev', split_axis=0, concat_axis=0, tiled=True)  8.42 us
  transfers between devices with their start and end apart: 5, of which 4 were waited for; matrix products, arithmetic and copies ran while one was open for 0% of the time, Pallas kernels for 0%

commit v1 on v0

--- a/solution.py
+++ b/solution.py
@@ -1,3 +1,4 @@
+import functools
 import jax
 import jax.numpy as jnp
 from jax import lax
@@ -10,6 +11,18 @@
 LMAX = 128
 CAP = 9
 epsilon = 1e-05
+
+
+def cut_rails(xx, dim_k):
+    windows = []
+    for _ in range(lax.axis_size("dev")):
+        windows.append(xx)
+    return jnp.concatenate(
+        lax.all_to_all(jnp.stack(windows), axis_name="dev", split_axis=0, concat_axis=0), axis=dim_k
+    )
+
+
+detail_series = functools.partial(cut_rails, dim_k=1)
 
 
 def from_behind(x, axis, by):
@@ -120,9 +133,7 @@
         jnp.float32
     )
     moved_rows, moved_high = from_behind((buffer, flat_h[:, half:]), "sec", 1)
-    mine = lax.dynamic_index_in_dim(
-        lax.all_gather(moved_rows, "dev", axis=1, tiled=True), my_expert, 0, keepdims=False
-    )
+    mine = lax.dynamic_index_in_dim(detail_series(moved_rows), my_expert, 0, keepdims=False)
     partials = lax.cond(
         is_expert,
         lambda block: expert_rows(block, w_gate, w_up, w_down),

time: 404 us -> 815 us (2.02); the launches traced: 403 us -> 805 us
  waiting for transfers between devices: 312 us -> 671 us
  starting transfers between devices: 12.3 us -> 59.3 us
  between operations: 13.5 us -> 0.15 us
  local copies, waits for them, and re-layouts: 35.4 us -> 46.4 us
    all_to_all x0 -> x1, waiting for transfers between devices: none -> 500 us  [cut_rails(): lax.all_to_all(jnp.stack(windows), axis_name='dev', split_axis=0, concat_...]
    all_gather x1 -> x0, waiting for transfers between devices: 144 us -> none  [shards(): lax.all_gather(moved_rows, 'dev', axis=1, tiled=True)]
    all_to_all x1, starting transfers between devices: 8.42 us -> 44.6 us  [shards(): lax.all_to_all(partials, 'dev', split_axis=0, concat_axis=0, tiled=True)]
    dynamic_slice x0 -> x1, local copies, waits for them, and re-layouts: none -> 17 us  [shards(): lax.dynamic_index_in_dim(detail_series(moved_rows), my_expert, 0, keepdim...]
    all_to_all x0 -> x1, starting transfers between devices: none -> 10.8 us  [cut_rails(): lax.all_to_all(jnp.stack(windows), axis_name='dev', split_axis=0, concat_...]
where the time goes in v1:
time: 815 us; the launch traced here: 805 us
  waiting for transfers between devices  671 us (82%)
  starting transfers between devices  59.3 us (7%)
  local copies, waits for them, and re-layouts  46.4 us (6%)
  matrix products  19.7 us (2%)
    all_to_all x1, waiting for transfers between devices, cut_rails(): lax.all_to_all(jnp.stack(windows), axis_name='dev', split_axis=0, concat_...  500 us
    all_to_all x1, waiting for transfers between devices, shards(): lax.all_to_all(partials, 'dev', split_axis=0, concat_axis=0, tiled=True)  158 us
    all_to_all x1, starting transfers between devices, shards(): lax.all_to_all(partials, 'dev', split_axis=0, concat_axis=0, tiled=True)  44.6 us
    dynamic_slice x1, local copies, waits for them, and re-layouts, shards(): lax.dynamic_index_in_dim(detail_series(moved_rows), my_expert, 0, keepdim...  17 us
  transfers between devices with their start and end apart: 5, of which 4 were waited for; matrix products, arithmetic and copies ran while one was open for 0% of the time, Pallas kernels for 0%

profile of v1, /device:TPU:25, one launch (start us, length us, event | category | flops | bytes accessed | tf_op | source)
XLA Modules:
  0.0 804.5 jit_solution(16311713717833972563)
XLA Ops:
  0.0 0.8 copy.60
  1.3 0.7 multiply_add_fusion
  2.0 0.8 conditional.2
  2.0 0.7 broadcast.104
  3.8 1.3 collective-permute-start
  5.1 10.6 %collective-permute-done = bf16[4,9,6144]{2,0,1:T(4,128)(2,1)S(1)} collective-permute-done((bf16[4,9,6144]{2,0,1:T(4,128)(2,1)S(1)}, bf16[4,9,6144]{2,0,1:T(4,128)(2,1)S(1)}, u32[]{:S(2)}, u32[]{:S(2)}) %collective-permute-start) | collective-permute-done | bytes 442400 | tf_op jit(solution)/shard_map/ppermute | solution.py:31
  15.6 15.0 %stack.2 = bf16[64,4,9,6144]{3,1,2,0:T(4,128)(2,1)} broadcast(bf16[4,9,6144]{2,0,1:T(4,128)(2,1)S(1)} %collective-permute-done), dimensions={1,2,3} | broadcast | bytes 28753920 | tf_op jit(solution)/shard_map/stack | solution.py:21
  30.6 10.8 %all-to-all-start = ((bf16[64,4,9,6144]{3,1,2,0:T(4,128)(2,1)}), bf16[64,4,9,6144]{3,1,2,0:T(4,128)(2,1)}, u32[]{:S(2)}, u32[]{:S(2)}) async-start(bf16[64,4,9,6144]{3,1,2,0:T(4,128)(2,1)} %stack.2), calls=%async_computation | async-start | bytes 56623104 | tf_op jit(solution)/shard_map/all_to_all | solution.py:21
  41.4 500.4 %all-to-all-done = bf16[64,4,9,6144]{3,1,2,0:T(4,128)(2,1)} async-done(((bf16[64,4,9,6144]{3,1,2,0:T(4,128)(2,1)}), bf16[64,4,9,6144]{3,1,2,0:T(4,128)(2,1)}, u32[]{:S(2)}, u32[]{:S(2)}) %all-to-all-start) | async-done | bytes 28311584 | tf_op jit(solution)/shard_map/all_to_all | solution.py:21
  541.8 35.7 %conditional.3 = (bf16[576,6144]{1,0:T(8,128)(2,1)}) conditional(s32[]{:T(128)} %convert_element_type.63, () %tuple.38, (bf16[4,64,9,6144]{3,0,2,1:T(4,128)(2,1)}, s32[]{:T(128)}, s32[]{:T(128)}, s32[]{:T(128)}, bf16[6144,512]{1,0:T(8,128)(2,1)}, /*index=5*/bf16[6144,512]{1,0:T(8,128)(2,1)}, bf16[512,6144]{1,0:T(8,128)(2,1)}, s32[]{:T(128)}) %tuple.40), branch_computations={%region_9.10_spmd, %region_10.11_spmd.clone} | conditional | flops 10876944384 | bytes 101843216 | solution.py:137
  541.8 17.0 %constant_dynamic-slice_fusion = bf16[1,576,6144]{2,0,1:T(2,128)(2,1)S(1)} fusion(bf16[4,576,6144]{2,0,1:T(4,128)(2,1)} %bitcast.10, s32[]{:T(128)S(6)} %select_n.31), kind=kLoop, calls=%fused_computation.36 | loop fusion | bytes 14155780 | tf_op jit(solution)/shard_map/jit(dynamic_index_in_dim)/dynamic_slice | solution.py:136
  558.8 5.2 fusion.15
  564.0 7.6 fusion.22
  571.7 5.8 convolution_convert_fusion
  577.5 10.2 %reshape.136 = bf16[64,9,6144]{2,1,0:T(8,128)(2,1)} reshape(bf16[576,6144]{1,0:T(8,128)(2,1)} %get-tuple-element.220) | data formatting | bytes 14155776 | tf_op jit(solution)/shard_map/reshape | solution.py:143
  587.7 44.6 %all-to-all-start.1 = ((bf16[64,9,6144]{2,1,0:T(8,128)(2,1)}), bf16[64,9,6144]{2,1,0:T(8,128)(2,1)}, u32[]{:S(2)}, u32[]{:S(2)}) async-start(bf16[64,9,6144]{2,1,0:T(8,128)(2,1)} %reshape.136), calls=%async_computation.1 | async-start | bytes 25165824 | tf_op jit(solution)/shard_map/all_to_all | solution.py:144
  632.4 158.2 %all-to-all-done.1 = bf16[64,9,6144]{2,1,0:T(8,128)(2,1)} async-done(((bf16[64,9,6144]{2,1,0:T(8,128)(2,1)}), bf16[64,9,6144]{2,1,0:T(8,128)(2,1)}, u32[]{:S(2)}, u32[]{:S(2)}) %all-to-all-start.1) | async-done | bytes 7077920 | tf_op jit(solution)/shard_map/all_to_all | solution.py:144
  790.6 6.8 convert_reduce_fusion
  797.6 0.7 fusion.28
  798.3 1.3 collective-permute-start.1
  799.6 1.0 reshape.133
  800.6 1.3 collective-permute-start.2
  801.9 1.9 collective-permute-done.2
  803.8 0.7 reshape.138
  (29 shorter events, 1.8 us)
Async XLA Ops:
  3.8 11.8 %collective-permute-start = (bf16[4,9,6144]{2,0,1:T(4,128)(2,1)S(1)}, bf16[4,9,6144]{2,0,1:T(4,128)(2,1)S(1)}, u32[]{:S(2)}, u32[]{:S(2)}) collective-permute-start(bf16[4,9,6144]{2,0,1:T(4,128)(2,1)S(1)} %copy.62), channel_id=1, source_target_pairs={{0,64},{1,65},{2,66},{3,67},{4,68},{5,69},{6,70},{7,71},{8,72},{9,... | collective-permute-start | bytes 1327112 | tf_op jit(solution)/shard_map/ppermute | solution.py:31
  30.6 511.2 %all-to-all-start = ((bf16[64,4,9,6144]{3,1,2,0:T(4,128)(2,1)}), bf16[64,4,9,6144]{3,1,2,0:T(4,128)(2,1)}, u32[]{:S(2)}, u32[]{:S(2)}) async-start(bf16[64,4,9,6144]{3,1,2,0:T(4,128)(2,1)} %stack.2), calls=%async_computation | async-start | bytes 56623104 | tf_op jit(solution)/shard_map/all_to_all | solution.py:21
  541.8 17.0 %copy-start.4 = (bf16[6144,512]{1,0:T(8,128)(2,1)S(1)}, bf16[6144,512]{1,0:T(8,128)(2,1)}, u32[]{:S(2)}) copy-start(bf16[6144,512]{1,0:T(8,128)(2,1)} %get-tuple-element.191) | copy-start | bytes 18874372 | tf_op jit(solution)/shard_map/cond
  558.8 12.9 %slice-start = ((s8[6291456]{0:T(1024)(128)(4,1)}), s8[2097152]{0:T(1024)(128)(4,1)S(1)}, s32[]{:S(2)}) async-start(s8[6291456]{0:T(1024)(128)(4,1)} %bitcast.40), calls=%async_computation.2 | async-start | bytes 4194304 | tf_op jit(solution)/shard_map/cond
  564.0 7.7 slice-start.1
  587.7 44.6 %copy-start.3 = (f32[16,2]{0,1:T(2,128)S(1)}, f32[16,2]{0,1:T(2,128)}, u32[]{:S(2)}) copy-start(f32[16,2]{0,1:T(2,128)} %param.26) | copy-start | bytes 388
  587.7 202.9 %all-to-all-start.1 = ((bf16[64,9,6144]{2,1,0:T(8,128)(2,1)}), bf16[64,9,6144]{2,1,0:T(8,128)(2,1)}, u32[]{:S(2)}, u32[]{:S(2)}) async-start(bf16[64,9,6144]{2,1,0:T(8,128)(2,1)} %reshape.136), calls=%async_computation.1 | async-start | bytes 25165824 | tf_op jit(solution)/shard_map/all_to_all | solution.py:144
  798.3 5.5 collective-permute-start.1
  800.6 3.2 collective-permute-start.2
